TPU v7x, 32 devices: a whole 2x2x4 slice. The times are simulated.
32 devices in a mesh: groups: 1, blk: 16 (over z, y, core), pts: 2 (over x).
Axes of the slice: x: 2, y: 2, z: 4, core: 2. Of those that a mesh axis runs over, the one named last changes fastest.
Arguments:
- gen_points: float32 [16, 3, 1024], P(('groups', 'blk'), None, 'pts'), may hold values from -5 to 5, as said below
- ref_points: float32 [128, 3, 1024], P(('groups', 'blk'), None, 'pts'), may hold values from -5 to 5, as said below
Outputs:
- chamfer: float32 [16, 128], P(('groups', 'blk'))
Inputs may be any that keep to these rules, and one draw needn't show every extreme that they name: `gen_points`: each shape is a cloud of points around a centre of its own, with a spread of its own. `ref_points`: each shape is a cloud of points around a centre of its own, with a spread of its own.
All inputs are finite; a program needn't handle non-finite values.
Results may differ from a plain program's by a relative error of at most 0.00002.
Values sent between devices are 32-bit elements; how exact they have to be, the bound alone decides.
A program may use at most 64 MiB of HBM per device.

v0:
```python
import jax
import jax.numpy as jnp
from jax import lax
from jax.sharding import PartitionSpec as P


def block_width(count):
    width = 1
    for trial in range(1, 9):
        if count % trial == 0:
            width = trial
    return width


def over_blocks(shape_fn, piece):
    count = piece.shape[0]
    width = block_width(count)
    grouped = piece.reshape((count // width, width) + piece.shape[1:])
    results = lax.map(shape_fn, grouped)
    return jax.tree.map(lambda value: value.reshape((count,) + value.shape[2:]), results)


def shards(gen_points, ref_points):
    gen_full = lax.all_gather(gen_points, "pts", axis=2, tiled=True)
    gen_count = gen_full.shape[0]
    point_count = gen_full.shape[2]
    blk_count = lax.axis_size("blk")
    ref_total = ref_points.shape[0] * blk_count

    def distances(shape_block):
        diff_x = gen_full[None, :, 0, :, None] - shape_block[:, None, 0, None, :]
        diff_y = gen_full[None, :, 1, :, None] - shape_block[:, None, 1, None, :]
        diff_z = gen_full[None, :, 2, :, None] - shape_block[:, None, 2, None, :]
        return diff_x * diff_x + diff_y * diff_y + diff_z * diff_z

    def some_shapes(shape_block):
        dist = distances(shape_block)
        return (jnp.min(dist, axis=3), jnp.sum(jnp.min(dist, axis=2), axis=2))

    near_block, far_block = over_blocks(
        some_shapes, lax.all_gather(ref_points, "blk", axis=0, tiled=True)
    )
    nearest = jnp.moveaxis(near_block, 0, 1)
    far_total = jnp.moveaxis(far_block, 0, 1)
    nearest, far_total = (nearest, far_total)
    shaped = nearest.reshape(gen_count, ref_total, 1, point_count)
    arrived = lax.all_to_all(shaped, "pts", split_axis=3, concat_axis=2, tiled=True)
    own_share = jnp.sum(jnp.min(arrived, axis=2), axis=2)
    near_all, far_all = lax.psum((own_share, far_total), "pts")
    return near_all / point_count + far_all / point_count


def solution(mesh):
    placed = (P(("groups", "blk"), None, "pts"), P(("groups", "blk"), None, "pts"))
    return jax.shard_map(
        shards, mesh=mesh, in_specs=placed, out_specs=P(("groups", "blk"), None), check_vma=False
    )
```

profile of v0, /device:TPU:0, one launch (start us, length us, event | category | flops | bytes accessed | tf_op | source)
XLA Modules:
  0.0 154.0 jit_solution(9465748119743954632)
XLA Ops:
  0.0 0.7 copy.18
  0.7 5.3 %all_gather.6 = f32[1,3,1024]{2,1,0:T(4,128)S(1)} all-gather(f32[1,3,512]{2,1,0:T(4,128)S(1)} %copy.18), channel_id=1, replica_groups=mesh['groups'=1,'blk'=16,'pts'=2] {'pts'}, dimensions={2}, use_global_device_ids=true | all-gather | bytes 18432 | tf_op jit(solution)/shard_map/all_gather | solution.py:24
  6.0 24.7 %all_gather.7 = f32[128,3,512]{2,0,1:T(8,128)S(1)} all-gather(f32[8,3,512]{2,0,1:T(8,128)} %param.5), channel_id=1, replica_groups=mesh['groups'=1,'blk'=16,'pts'=2] {'blk'}, dimensions={0}, use_global_device_ids=true | all-gather | bytes 835584 | tf_op jit(solution)/shard_map/all_gather | solution.py:41
  30.7 104.5 %while.12 = (s32[]{:T(128)}, f32[16,8,1,1024]{3,1,2,0:T(8,128)S(1)}, f32[16,8,1]{1,2,0:T(1,128)S(1)}, f32[1,3,1024]{2,1,0:T(4,128)S(1)}, f32[16,8,3,512]{3,1,0,2:T(8,128)S(1)}, /*index=5*/s32[]{:T(128)}, f32[]{:T(128)}) while((s32[]{:T(128)}, f32[16,8,1,1024]{3,1,2,0:T(8,128)S(1)}, f32[16,8,1]{1,2,0:T(1,128)S(1)}, ...), condition=%wide.region_4.5_spmd, body=%wide.region_0.4_spmd.sunk | while | flops 41934840 | bytes 414853 | solution.py:19
  30.8 6.3 %fusion.6 = (f32[8,512]{1,0:T(8,128)S(1)}, f32[8,1024]{1,0:T(8,128)S(1)}) fusion(f32[8,512]{1,0:T(8,128)S(1)} %get-tuple-element.97, f32[1024]{0:T(1024)S(1)} %bitcast.41, f32[8,512]{1,0:T(8,128)S(1)} %get-tuple-element.99, f32[1024]{0:T(1024)S(1)} %bitcast.42, f32[8,512]{1,0:T(8,128)S(1)} %get-tuple-element.101, f32[1024]{0:T(1024)S(1)} %bitcast.40), kind=kLoop, calls=%fused_computation.1.clone.1 | loop fusion | flops 41930752 | bytes 110592 | tf_op jit(solution)/shard_map/while/body/eval_jaxpr/reduce_min | solution.py:38
  37.1 0.1 reduce_sum.23
  37.3 6.3 %fusion.6 = (f32[8,512]{1,0:T(8,128)S(1)}, f32[8,1024]{1,0:T(8,128)S(1)}) fusion(f32[8,512]{1,0:T(8,128)S(1)} %get-tuple-element.97, f32[1024]{0:T(1024)S(1)} %bitcast.41, f32[8,512]{1,0:T(8,128)S(1)} %get-tuple-element.99, f32[1024]{0:T(1024)S(1)} %bitcast.42, f32[8,512]{1,0:T(8,128)S(1)} %get-tuple-element.101, f32[1024]{0:T(1024)S(1)} %bitcast.40), kind=kLoop, calls=%fused_computation.1.clone.1 | loop fusion | flops 41930752 | bytes 110592 | tf_op jit(solution)/shard_map/while/body/eval_jaxpr/reduce_min | solution.py:38
  43.6 0.1 reduce_sum.23
  43.8 6.3 %fusion.6 = (f32[8,512]{1,0:T(8,128)S(1)}, f32[8,1024]{1,0:T(8,128)S(1)}) fusion(f32[8,512]{1,0:T(8,128)S(1)} %get-tuple-element.97, f32[1024]{0:T(1024)S(1)} %bitcast.41, f32[8,512]{1,0:T(8,128)S(1)} %get-tuple-element.99, f32[1024]{0:T(1024)S(1)} %bitcast.42, f32[8,512]{1,0:T(8,128)S(1)} %get-tuple-element.101, f32[1024]{0:T(1024)S(1)} %bitcast.40), kind=kLoop, calls=%fused_computation.1.clone.1 | loop fusion | flops 41930752 | bytes 110592 | tf_op jit(solution)/shard_map/while/body/eval_jaxpr/reduce_min | solution.py:38
  50.1 0.1 reduce_sum.23
  50.3 6.3 %fusion.6 = (f32[8,512]{1,0:T(8,128)S(1)}, f32[8,1024]{1,0:T(8,128)S(1)}) fusion(f32[8,512]{1,0:T(8,128)S(1)} %get-tuple-element.97, f32[1024]{0:T(1024)S(1)} %bitcast.41, f32[8,512]{1,0:T(8,128)S(1)} %get-tuple-element.99, f32[1024]{0:T(1024)S(1)} %bitcast.42, f32[8,512]{1,0:T(8,128)S(1)} %get-tuple-element.101, f32[1024]{0:T(1024)S(1)} %bitcast.40), kind=kLoop, calls=%fused_computation.1.clone.1 | loop fusion | flops 41930752 | bytes 110592 | tf_op jit(solution)/shard_map/while/body/eval_jaxpr/reduce_min | solution.py:38
  56.7 0.1 reduce_sum.23
  56.9 6.3 %fusion.6 = (f32[8,512]{1,0:T(8,128)S(1)}, f32[8,1024]{1,0:T(8,128)S(1)}) fusion(f32[8,512]{1,0:T(8,128)S(1)} %get-tuple-element.97, f32[1024]{0:T(1024)S(1)} %bitcast.41, f32[8,512]{1,0:T(8,128)S(1)} %get-tuple-element.99, f32[1024]{0:T(1024)S(1)} %bitcast.42, f32[8,512]{1,0:T(8,128)S(1)} %get-tuple-element.101, f32[1024]{0:T(1024)S(1)} %bitcast.40), kind=kLoop, calls=%fused_computation.1.clone.1 | loop fusion | flops 41930752 | bytes 110592 | tf_op jit(solution)/shard_map/while/body/eval_jaxpr/reduce_min | solution.py:38
  63.2 0.1 reduce_sum.23
  63.4 6.3 %fusion.6 = (f32[8,512]{1,0:T(8,128)S(1)}, f32[8,1024]{1,0:T(8,128)S(1)}) fusion(f32[8,512]{1,0:T(8,128)S(1)} %get-tuple-element.97, f32[1024]{0:T(1024)S(1)} %bitcast.41, f32[8,512]{1,0:T(8,128)S(1)} %get-tuple-element.99, f32[1024]{0:T(1024)S(1)} %bitcast.42, f32[8,512]{1,0:T(8,128)S(1)} %get-tuple-element.101, f32[1024]{0:T(1024)S(1)} %bitcast.40), kind=kLoop, calls=%fused_computation.1.clone.1 | loop fusion | flops 41930752 | bytes 110592 | tf_op jit(solution)/shard_map/while/body/eval_jaxpr/reduce_min | solution.py:38
  69.9 6.3 %fusion.6 = (f32[8,512]{1,0:T(8,128)S(1)}, f32[8,1024]{1,0:T(8,128)S(1)}) fusion(f32[8,512]{1,0:T(8,128)S(1)} %get-tuple-element.97, f32[1024]{0:T(1024)S(1)} %bitcast.41, f32[8,512]{1,0:T(8,128)S(1)} %get-tuple-element.99, f32[1024]{0:T(1024)S(1)} %bitcast.42, f32[8,512]{1,0:T(8,128)S(1)} %get-tuple-element.101, f32[1024]{0:T(1024)S(1)} %bitcast.40), kind=kLoop, calls=%fused_computation.1.clone.1 | loop fusion | flops 41930752 | bytes 110592 | tf_op jit(solution)/shard_map/while/body/eval_jaxpr/reduce_min | solution.py:38
  76.5 6.3 %fusion.6 = (f32[8,512]{1,0:T(8,128)S(1)}, f32[8,1024]{1,0:T(8,128)S(1)}) fusion(f32[8,512]{1,0:T(8,128)S(1)} %get-tuple-element.97, f32[1024]{0:T(1024)S(1)} %bitcast.41, f32[8,512]{1,0:T(8,128)S(1)} %get-tuple-element.99, f32[1024]{0:T(1024)S(1)} %bitcast.42, f32[8,512]{1,0:T(8,128)S(1)} %get-tuple-element.101, f32[1024]{0:T(1024)S(1)} %bitcast.40), kind=kLoop, calls=%fused_computation.1.clone.1 | loop fusion | flops 41930752 | bytes 110592 | tf_op jit(solution)/shard_map/while/body/eval_jaxpr/reduce_min | solution.py:38
  83.0 6.3 %fusion.6 = (f32[8,512]{1,0:T(8,128)S(1)}, f32[8,1024]{1,0:T(8,128)S(1)}) fusion(f32[8,512]{1,0:T(8,128)S(1)} %get-tuple-element.97, f32[1024]{0:T(1024)S(1)} %bitcast.41, f32[8,512]{1,0:T(8,128)S(1)} %get-tuple-element.99, f32[1024]{0:T(1024)S(1)} %bitcast.42, f32[8,512]{1,0:T(8,128)S(1)} %get-tuple-element.101, f32[1024]{0:T(1024)S(1)} %bitcast.40), kind=kLoop, calls=%fused_computation.1.clone.1 | loop fusion | flops 41930752 | bytes 110592 | tf_op jit(solution)/shard_map/while/body/eval_jaxpr/reduce_min | solution.py:38
  89.5 6.3 %fusion.6 = (f32[8,512]{1,0:T(8,128)S(1)}, f32[8,1024]{1,0:T(8,128)S(1)}) fusion(f32[8,512]{1,0:T(8,128)S(1)} %get-tuple-element.97, f32[1024]{0:T(1024)S(1)} %bitcast.41, f32[8,512]{1,0:T(8,128)S(1)} %get-tuple-element.99, f32[1024]{0:T(1024)S(1)} %bitcast.42, f32[8,512]{1,0:T(8,128)S(1)} %get-tuple-element.101, f32[1024]{0:T(1024)S(1)} %bitcast.40), kind=kLoop, calls=%fused_computation.1.clone.1 | loop fusion | flops 41930752 | bytes 110592 | tf_op jit(solution)/shard_map/while/body/eval_jaxpr/reduce_min | solution.py:38
  96.1 6.3 %fusion.6 = (f32[8,512]{1,0:T(8,128)S(1)}, f32[8,1024]{1,0:T(8,128)S(1)}) fusion(f32[8,512]{1,0:T(8,128)S(1)} %get-tuple-element.97, f32[1024]{0:T(1024)S(1)} %bitcast.41, f32[8,512]{1,0:T(8,128)S(1)} %get-tuple-element.99, f32[1024]{0:T(1024)S(1)} %bitcast.42, f32[8,512]{1,0:T(8,128)S(1)} %get-tuple-element.101, f32[1024]{0:T(1024)S(1)} %bitcast.40), kind=kLoop, calls=%fused_computation.1.clone.1 | loop fusion | flops 41930752 | bytes 110592 | tf_op jit(solution)/shard_map/while/body/eval_jaxpr/reduce_min | solution.py:38
  102.6 6.3 %fusion.6 = (f32[8,512]{1,0:T(8,128)S(1)}, f32[8,1024]{1,0:T(8,128)S(1)}) fusion(f32[8,512]{1,0:T(8,128)S(1)} %get-tuple-element.97, f32[1024]{0:T(1024)S(1)} %bitcast.41, f32[8,512]{1,0:T(8,128)S(1)} %get-tuple-element.99, f32[1024]{0:T(1024)S(1)} %bitcast.42, f32[8,512]{1,0:T(8,128)S(1)} %get-tuple-element.101, f32[1024]{0:T(1024)S(1)} %bitcast.40), kind=kLoop, calls=%fused_computation.1.clone.1 | loop fusion | flops 41930752 | bytes 110592 | tf_op jit(solution)/shard_map/while/body/eval_jaxpr/reduce_min | solution.py:38
  109.1 6.3 %fusion.6 = (f32[8,512]{1,0:T(8,128)S(1)}, f32[8,1024]{1,0:T(8,128)S(1)}) fusion(f32[8,512]{1,0:T(8,128)S(1)} %get-tuple-element.97, f32[1024]{0:T(1024)S(1)} %bitcast.41, f32[8,512]{1,0:T(8,128)S(1)} %get-tuple-element.99, f32[1024]{0:T(1024)S(1)} %bitcast.42, f32[8,512]{1,0:T(8,128)S(1)} %get-tuple-element.101, f32[1024]{0:T(1024)S(1)} %bitcast.40), kind=kLoop, calls=%fused_computation.1.clone.1 | loop fusion | flops 41930752 | bytes 110592 | tf_op jit(solution)/shard_map/while/body/eval_jaxpr/reduce_min | solution.py:38
  115.6 6.3 %fusion.6 = (f32[8,512]{1,0:T(8,128)S(1)}, f32[8,1024]{1,0:T(8,128)S(1)}) fusion(f32[8,512]{1,0:T(8,128)S(1)} %get-tuple-element.97, f32[1024]{0:T(1024)S(1)} %bitcast.41, f32[8,512]{1,0:T(8,128)S(1)} %get-tuple-element.99, f32[1024]{0:T(1024)S(1)} %bitcast.42, f32[8,512]{1,0:T(8,128)S(1)} %get-tuple-element.101, f32[1024]{0:T(1024)S(1)} %bitcast.40), kind=kLoop, calls=%fused_computation.1.clone.1 | loop fusion | flops 41930752 | bytes 110592 | tf_op jit(solution)/shard_map/while/body/eval_jaxpr/reduce_min | solution.py:38
  122.2 6.3 %fusion.6 = (f32[8,512]{1,0:T(8,128)S(1)}, f32[8,1024]{1,0:T(8,128)S(1)}) fusion(f32[8,512]{1,0:T(8,128)S(1)} %get-tuple-element.97, f32[1024]{0:T(1024)S(1)} %bitcast.41, f32[8,512]{1,0:T(8,128)S(1)} %get-tuple-element.99, f32[1024]{0:T(1024)S(1)} %bitcast.42, f32[8,512]{1,0:T(8,128)S(1)} %get-tuple-element.101, f32[1024]{0:T(1024)S(1)} %bitcast.40), kind=kLoop, calls=%fused_computation.1.clone.1 | loop fusion | flops 41930752 | bytes 110592 | tf_op jit(solution)/shard_map/while/body/eval_jaxpr/reduce_min | solution.py:38
  128.7 6.3 %fusion.6 = (f32[8,512]{1,0:T(8,128)S(1)}, f32[8,1024]{1,0:T(8,128)S(1)}) fusion(f32[8,512]{1,0:T(8,128)S(1)} %get-tuple-element.97, f32[1024]{0:T(1024)S(1)} %bitcast.41, f32[8,512]{1,0:T(8,128)S(1)} %get-tuple-element.99, f32[1024]{0:T(1024)S(1)} %bitcast.42, f32[8,512]{1,0:T(8,128)S(1)} %get-tuple-element.101, f32[1024]{0:T(1024)S(1)} %bitcast.40), kind=kLoop, calls=%fused_computation.1.clone.1 | loop fusion | flops 41930752 | bytes 110592 | tf_op jit(solution)/shard_map/while/body/eval_jaxpr/reduce_min | solution.py:38
  135.2 1.0 copy.20
  136.2 3.5 %all-to-all-start = ((f32[1,128,1,1024]{1,2,0,3:T(1,128)}), f32[1,128,1,1024]{1,2,0,3:T(1,128)S(1)}, u32[]{:S(2)}, u32[]{:S(2)}) async-start(f32[1,128,1,1024]{1,2,0,3:T(1,128)} %copy.20), calls=%async_computation | async-start | bytes 1048576 | tf_op jit(solution)/shard_map/all_to_all | solution.py:47
  139.7 0.5 broadcast.64
  140.2 0.7 reduce.13
  141.0 7.5 %all-to-all-done = f32[1,128,1,1024]{1,2,0,3:T(1,128)S(1)} async-done(((f32[1,128,1,1024]{1,2,0,3:T(1,128)}), f32[1,128,1,1024]{1,2,0,3:T(1,128)S(1)}, u32[]{:S(2)}, u32[]{:S(2)}) %all-to-all-start) | async-done | bytes 524320 | tf_op jit(solution)/shard_map/all_to_all | solution.py:47
  148.6 4.9 %psum.16 = f32[1,128]{1,0:T(1,128)S(1)} all-reduce(f32[1,128]{1,0:T(1,128)S(1)} %bitcast_add_fusion), channel_id=1, replica_groups=mesh['groups'=1,'blk'=16,'pts'=2] {'pts'}, use_global_device_ids=true, to_apply=%region_7.8 | all-reduce | flops 128 | bytes 1024 | tf_op jit(solution)/shard_map/psum | solution.py:49
  153.5 0.5 broadcast_multiply_fusion
  (97 shorter events, 2.2 us)
Async XLA Ops:
  136.2 12.2 %all-to-all-start = ((f32[1,128,1,1024]{1,2,0,3:T(1,128)}), f32[1,128,1,1024]{1,2,0,3:T(1,128)S(1)}, u32[]{:S(2)}, u32[]{:S(2)}) async-start(f32[1,128,1,1024]{1,2,0,3:T(1,128)} %copy.20), calls=%async_computation | async-start | bytes 1048576 | tf_op jit(solution)/shard_map/all_to_all | solution.py:47
where the time goes:
time: 154 us
  other arithmetic  104 us (68%)
  blocking collectives  34.9 us (23%)
  waiting for transfers between devices  7.48 us (5%)
  starting transfers between devices  3.49 us (2%)
  local copies, waits for them, and re-layouts  3.05 us (2%)
    reduce_min x16, other arithmetic, some_shapes(): return (jnp.min(dist, axis=3), jnp.sum(jnp.min(dist, axis=2), axis=2))  101 us
    all_gather x1, blocking collectives, shards(): lax.all_gather(ref_points, 'blk', axis=0, tiled=True)  24.7 us
    all_to_all x1, waiting for transfers between devices, shards(): lax.all_to_all(shaped, 'pts', split_axis=3, concat_axis=2, tiled=True)  7.48 us
    all_gather x1, blocking collectives, shards(): gen_full = lax.all_gather(gen_points, 'pts', axis=2, tiled=True)  5.27 us
    psum x1, blocking collectives, shards(): near_all, far_all = lax.psum((own_share, far_total), 'pts')  4.93 us
    all_to_all x1, starting transfers between devices, shards(): lax.all_to_all(shaped, 'pts', split_axis=3, concat_axis=2, tiled=True)  3.49 us
  transfers between devices with their start and end apart: 1, of which 1 were waited for; matrix products, arithmetic and copies ran while one was open for 1% of the time, Pallas kernels for 0%

commit v1 on v0

v1 whole, which is shorter than its diff:
```python
import functools

import jax
import jax.numpy as jnp
from jax import lax
from jax.experimental import pallas as pl
from jax.experimental.pallas import tpu as pltpu
from jax.sharding import PartitionSpec as P

MESH = pl.DeviceIdType.MESH

DEPTH = 48


def split3(value):
    high = value.astype(jnp.bfloat16).astype(jnp.float32)
    middle = (value - high).astype(jnp.bfloat16).astype(jnp.float32)
    return high, middle, value - high - middle


def gen_rows(points, norm):
    n = points.shape[1]
    one, zero = jnp.ones((1, n), jnp.float32), jnp.zeros((1, n), jnp.float32)
    ph, pm, pl_ = split3(points)
    nh, nm, nl = split3(norm)
    tile = lambda p, c, q: jnp.concatenate([p, c, q, jnp.zeros((3, n), jnp.float32)], axis=0)
    stack = [
        tile(ph, one, nh), tile(pm, zero, nm), tile(pl_, zero, nl),
        tile(ph, one, zero), tile(pm, zero, zero), tile(ph, one, zero),
        jnp.zeros((128 - DEPTH, n), jnp.float32),
    ]
    return jnp.concatenate(stack, axis=0).T.astype(jnp.bfloat16)


def ref_rows(doubled, norm):
    n = doubled.shape[1]
    rows = jnp.concatenate([doubled, norm, jnp.ones((1, n), jnp.float32), jnp.zeros((3, n), jnp.float32)], axis=0)
    h, m, l = split3(rows)
    return jnp.concatenate([h, h, h, m, m, l], axis=0).astype(jnp.bfloat16)


def spread_gen(points, norm):
    count = points.shape[1]
    stack = jnp.concatenate([points, norm, jnp.zeros((124, count), jnp.float32)], axis=0).T
    return [jnp.broadcast_to(stack[:, c : c + 1], (count, 128)) for c in range(4)]


def pair_sums(rows_ref, gen, cols, wide_gen, wide_ref, n, mc, nc, vec):
    fsum = jnp.zeros((8, 128), jnp.float32)
    blocks = n // 128
    back = [None] * blocks
    chunks = (n - vec) // mc
    vec_tiles = vec // 8
    wide_back = [None] * blocks
    done = 0
    for ic in range(chunks):
        a = rows_ref[pl.ds(gen * n + ic * mc, mc), 0:DEPTH]
        acc = None
        for jc in range(n // nc):
            d = jnp.dot(a, cols[:, jc * nc : (jc + 1) * nc], preferred_element_type=jnp.float32)
            for q in range(nc // 128):
                part = d[:, q * 128 : (q + 1) * 128]
                acc = part if acc is None else jnp.minimum(acc, part)
                k = jc * (nc // 128) + q
                down = jnp.min(part.reshape(mc // 8, 8, 128), axis=0)
                back[k] = down if back[k] is None else jnp.minimum(back[k], down)
        near = jnp.broadcast_to(jnp.min(acc, axis=1, keepdims=True), (mc, 128))
        fsum = fsum + jnp.sum(near.reshape(mc // 8, 8, 128), axis=0)
        upto = vec_tiles * (ic + 1) // chunks
        for tile in range(done, upto):
            ax, ay, az, an = (wide_gen[gen, c, pl.ds(tile * 8, 8), :] for c in range(4))
            acc = None
            for k in range(blocks):
                bx, by, bz, bn = (wide_ref[c, :, pl.ds(k * 128, 128)] for c in range(4))
                cross = ax * bx + ay * by + az * bz
                u = cross + bn
                w = cross + an
                acc = u if acc is None else jnp.minimum(acc, u)
                wide_back[k] = w if wide_back[k] is None else jnp.minimum(wide_back[k], w)
            fsum = fsum + jnp.broadcast_to(jnp.min(acc, axis=1, keepdims=True), (8, 128)) + an
        done = upto
    far = None
    for k in range(blocks):
        down = back[k]
        if vec:
            down = jnp.minimum(down, wide_back[k] + wide_ref[3, :, pl.ds(k * 128, 128)])
        low = jnp.min(down, axis=0, keepdims=True)
        far = low if far is None else far + low
    return jnp.sum(fsum, axis=0, keepdims=True) + jnp.sum(far, axis=1, keepdims=True)


def kernel(sizes, gen_ref, ref_ref, out_ref, gbuf, rbuf, rows, wide_gen, wide_ref, res, obuf, g_send, g_recv, r_send, r_recv, o_send, o_recv):
    outer, inner, halves, chunk, n, mc, nc, vec = sizes
    blk, x = lax.axis_index("blk"), lax.axis_index("pts")
    bo, bi = blk // inner, blk % inner
    width = res.shape[2]
    plane = [(i, h) for i in range(inner) for h in range(halves) if (i, h) != (0, 0)]
    column = [(o, h) for o in range(outer) for h in range(halves) if (o, h) != (0, 0)]

    def plane_id(i, h):
        return lax.rem(bi + i, inner), lax.rem(x + h, halves)

    def column_id(o, h):
        return lax.rem(bo + o, outer), lax.rem(x + h, halves)

    barrier = pltpu.get_barrier_semaphore()
    for i, h in plane:
        ti, th = plane_id(i, h)
        pl.semaphore_signal(barrier, device_id={"blk": bo * inner + ti, "pts": th}, device_id_type=MESH)
    for o, h in column:
        if o:
            to, th = column_id(o, h)
            pl.semaphore_signal(barrier, device_id={"blk": to * inner + bi, "pts": th}, device_id_type=MESH)
    pl.semaphore_wait(barrier, len(plane) + len(column) - (halves - 1))

    copies = []
    for s, (i, h) in enumerate(plane):
        ti, th = plane_id(i, h)
        copies.append(
            pltpu.make_async_remote_copy(
                src_ref=gen_ref.at[0], dst_ref=gbuf.at[bi, x], send_sem=g_send.at[s], recv_sem=g_recv.at[bi, x],
                device_id={"blk": bo * inner + ti, "pts": th}, device_id_type=MESH,
            )
        )
    for s, (o, h) in enumerate(column):
        to, th = column_id(o, h)
        copies.append(
            pltpu.make_async_remote_copy(
                src_ref=ref_ref.at[pl.ds(th * chunk, chunk)], dst_ref=rbuf.at[bo, x], send_sem=r_send.at[s],
                recv_sem=r_recv.at[bo, x], device_id={"blk": to * inner + bi, "pts": th}, device_id_type=MESH,
            )
        )
    for copy in copies:
        copy.start()
    own_gen = pltpu.make_async_copy(gen_ref.at[0], gbuf.at[bi, x], g_recv.at[bi, x])
    own_ref = pltpu.make_async_copy(ref_ref.at[pl.ds(x * chunk, chunk)], rbuf.at[bo, x], r_recv.at[bo, x])
    own_gen.start()
    own_ref.start()

    for i in range(inner):
        for h in range(halves):
            pltpu.make_async_copy(gen_ref.at[0], gbuf.at[i, h], g_recv.at[i, h]).wait()
    for i in range(inner):
        points = jnp.concatenate([gbuf[i, h] for h in range(halves)], axis=1)
        norm = jnp.sum(points * points, axis=0, keepdims=True)
        rows[pl.ds(i * n, n), :] = gen_rows(points, norm)
        if vec:
            for c, wide in enumerate(spread_gen(points[:, n - vec :], norm[:, n - vec :])):
                wide_gen[i, c] = wide
    res[...] = jnp.zeros_like(res)
    lane = lax.broadcasted_iota(jnp.int32, (8, width), 1)

    def some_refs(step, carry):
        o = lax.rem(bo + step, outer)
        for h in range(halves):
            pltpu.make_async_copy(ref_ref.at[pl.ds(0, chunk)], rbuf.at[o, h], r_recv.at[o, h]).wait()

        def one_ref(c, carry):
            points = jnp.concatenate([rbuf[o, h, c] for h in range(halves)], axis=1)
            norm = jnp.sum(points * points, axis=0, keepdims=True)
            points = -2.0 * points
            cols = ref_rows(points, norm)
            if vec:
                for k in range(3):
                    wide_ref[k] = jnp.broadcast_to(points[k : k + 1], (8, n))
                wide_ref[3] = jnp.broadcast_to(norm, (8, n))
            place = lane == (o * inner + bi) * chunk * halves + x * chunk + c
            for i in range(inner):
                value = pair_sums(rows, i, cols, wide_gen, wide_ref, n, mc, nc, vec) * (1.0 / n)
                value = jnp.concatenate([value] * (width // 128), axis=1)
                res[i] = jnp.where(place, jnp.broadcast_to(value, (8, width)), res[i])
            return carry

        return lax.fori_loop(0, chunk, one_ref, carry)

    lax.fori_loop(0, outer, some_refs, 0)

    answers = []
    for s, (i, h) in enumerate(plane):
        ti, th = plane_id(i, h)
        answers.append(
            pltpu.make_async_remote_copy(
                src_ref=res.at[ti], dst_ref=obuf.at[bi, x], send_sem=o_send.at[s], recv_sem=o_recv.at[bi, x],
                device_id={"blk": bo * inner + ti, "pts": th}, device_id_type=MESH,
            )
        )
    for copy in answers:
        copy.start()
    total = res[bi]
    for i, h in plane:
        ti, th = plane_id(i, h)
        pltpu.make_async_copy(res.at[0], obuf.at[ti, th], o_recv.at[ti, th]).wait()
        total = total + obuf[ti, th]
    out_ref[...] = total[0:1]
    for copy in copies:
        copy.wait_send()
    for copy in answers:
        copy.wait_send()


def split_of(blk_count, pts_count, refs):
    for inner in (4, 2, 1):
        if blk_count % inner == 0:
            return blk_count // inner, inner


def shards(gen_points, ref_points):
    halves, blk_count = lax.axis_size("pts"), lax.axis_size("blk")
    refs, _, share = ref_points.shape
    n = share * halves
    outer, inner = split_of(blk_count, halves, refs)
    chunk = refs // halves
    width = refs * blk_count
    vec = 0
    sizes = (outer, inner, halves, chunk, n, 256, 256, vec)
    return pl.pallas_call(
        functools.partial(kernel, sizes),
        out_shape=jax.ShapeDtypeStruct((1, width), jnp.float32),
        in_specs=[pl.BlockSpec(memory_space=pltpu.VMEM)] * 2,
        out_specs=pl.BlockSpec(memory_space=pltpu.VMEM),
        scratch_shapes=[
            pltpu.VMEM((inner, halves, 3, share), jnp.float32),
            pltpu.VMEM((outer, halves, chunk, 3, share), jnp.float32),
            pltpu.VMEM((inner * n, 128), jnp.bfloat16),
            pltpu.VMEM((inner, 4, max(vec, 8), 128), jnp.float32),
            pltpu.VMEM((4, 8, n), jnp.float32),
            pltpu.VMEM((inner, 8, width), jnp.float32),
            pltpu.VMEM((inner, halves, 8, width), jnp.float32),
            pltpu.SemaphoreType.DMA((inner * halves,)),
            pltpu.SemaphoreType.DMA((inner, halves)),
            pltpu.SemaphoreType.DMA((outer * halves,)),
            pltpu.SemaphoreType.DMA((outer, halves)),
            pltpu.SemaphoreType.DMA((inner * halves,)),
            pltpu.SemaphoreType.DMA((inner, halves)),
        ],
        compiler_params=pltpu.CompilerParams(collective_id=0, has_side_effects=True),
        name="chamfer",
    )(gen_points, ref_points)


def solution(mesh):
    placed = (P(("groups", "blk"), None, "pts"), P(("groups", "blk"), None, "pts"))
    return jax.shard_map(
        shards, mesh=mesh, in_specs=placed, out_specs=P(("groups", "blk"), None), check_vma=False
    )
```

time: 154 us -> 58.2 us (0.38)
  other arithmetic: 104 us -> 0 us
  Pallas kernels: 0 us -> 54.1 us
  blocking collectives: 34.9 us -> 0 us
  waiting for transfers between devices: 7.48 us -> 0 us
  starting transfers between devices: 3.49 us -> 0 us
    reduce_min x17 -> x0, other arithmetic: 101 us -> none  [the longest x16 101 us: some_shapes(): return (jnp.min(dist, axis=3), jnp.sum(jnp.min(dist, axis=2), axis=2))]
    pallas_call x0 -> x1, Pallas kernels: none -> 54.1 us  [shards(): pl.pallas_call(functools.partial(kernel, sizes), out_shape=jax.ShapeDtype...]
    all_gather x2 -> x0, blocking collectives: 30 us -> none  [the longest x1 24.7 us: shards(): lax.all_gather(ref_points, 'blk', axis=0, tiled=True)]
    all_to_all x1 -> x0, waiting for transfers between devices: 7.48 us -> none  [shards(): lax.all_to_all(shaped, 'pts', split_axis=3, concat_axis=2, tiled=True)]
    psum x1 -> x0, blocking collectives: 4.93 us -> none  [shards(): near_all, far_all = lax.psum((own_share, far_total), 'pts')]
    all_to_all x1 -> x0, starting transfers between devices: 3.49 us -> none  [shards(): lax.all_to_all(shaped, 'pts', split_axis=3, concat_axis=2, tiled=True)]
    unnamed x1 -> x3, local copies, waits for them, and re-layouts: 0.69 us -> 3.86 us
    reduce_sum x17 -> x0, other arithmetic: 1.99 us -> none  [the longest x16 1.91 us: some_shapes(): return (jnp.min(dist, axis=3), jnp.sum(jnp.min(dist, axis=2), axis=2))]
  transfers between devices with their start and end apart: 1 -> 0, of which waited for: 1 -> 0; matrix products, arithmetic and copies ran while one was open for 1% -> 0% of each run, Pallas kernels for 0% -> 0%
where the time goes in v1:
time: 58.2 us; the launch traced here: 58 us
  Pallas kernels  54.1 us (93%)
  local copies, waits for them, and re-layouts  3.86 us (7%)
    pallas_call x1, Pallas kernels, shards(): pl.pallas_call(functools.partial(kernel, sizes), out_shape=jax.ShapeDtype...  54.1 us
    unnamed x3, local copies, waits for them, and re-layouts  3.86 us

profile of v1, /device:TPU:0, one launch (start us, length us, event | category | flops | bytes accessed | tf_op | source)
XLA Modules:
  0.0 58.0 jit_solution(1804783373124956428)
XLA Ops:
  0.0 1.3 %copy.3.gen_ref = f32[1,3,512]{2,1,0:T(4,128)} copy(f32[1,3,512]{2,0,1:T(1,128)} %param.2) | data formatting | bytes 12288 | tf_op args[0]
  1.3 1.5 %copy.4.ref_ref = f32[8,3,512]{2,1,0:T(4,128)} copy(f32[8,3,512]{2,0,1:T(8,128)} %param.3) | data formatting | bytes 98304 | tf_op args[1]
  2.7 54.1 %chamfer.1 = f32[1,128]{1,0:T(1,128)} custom-call(f32[1,3,512]{2,1,0:T(4,128)} %copy.3.gen_ref, f32[8,3,512]{2,1,0:T(4,128)} %copy.4.ref_ref), custom_call_target="tpu_custom_call" | custom-call | tf_op jit(solution)/shard_map/chamfer/pallas_call | solution.py:216
  56.9 1.1 %copy.6 = f32[1,128]{1,0:T(1,128)} copy(f32[1,128]{1,0:T(1,128)} %chamfer.1) | data formatting | bytes 1024

commit v2 on v1

--- a/solution.py
+++ b/solution.py
@@ -89,7 +89,7 @@
     return jnp.sum(fsum, axis=0, keepdims=True) + jnp.sum(far, axis=1, keepdims=True)
 
 
-def kernel(sizes, gen_ref, ref_ref, out_ref, gbuf, rbuf, rows, wide_gen, wide_ref, res, obuf, g_send, g_recv, r_send, r_recv, o_send, o_recv):
+def kernel(sizes, gen_in, ref_in, out_ref, gen_ref, ref_ref, gbuf, rbuf, rows, wide_gen, wide_ref, res, obuf, g_send, g_recv, r_send, r_recv, o_send, o_recv):
     outer, inner, halves, chunk, n, mc, nc, vec = sizes
     blk, x = lax.axis_index("blk"), lax.axis_index("pts")
     bo, bi = blk // inner, blk % inner
@@ -102,6 +102,11 @@
 
     def column_id(o, h):
         return lax.rem(bo + o, outer), lax.rem(x + h, halves)
+
+    for k in range(3):
+        gen_ref[0, k : k + 1, :] = gen_in[k]
+        for c in range(halves * chunk):
+            ref_ref[c // chunk, c % chunk, k : k + 1, :] = ref_in[k, c : c + 1, :]
 
     barrier = pltpu.get_barrier_semaphore()
     for i, h in plane:
@@ -126,24 +131,24 @@
         to, th = column_id(o, h)
         copies.append(
             pltpu.make_async_remote_copy(
-                src_ref=ref_ref.at[pl.ds(th * chunk, chunk)], dst_ref=rbuf.at[bo, x], send_sem=r_send.at[s],
+                src_ref=ref_ref.at[th], dst_ref=rbuf.at[bo, x], send_sem=r_send.at[s],
                 recv_sem=r_recv.at[bo, x], device_id={"blk": to * inner + bi, "pts": th}, device_id_type=MESH,
             )
         )
     for copy in copies:
         copy.start()
     own_gen = pltpu.make_async_copy(gen_ref.at[0], gbuf.at[bi, x], g_recv.at[bi, x])
-    own_ref = pltpu.make_async_copy(ref_ref.at[pl.ds(x * chunk, chunk)], rbuf.at[bo, x], r_recv.at[bo, x])
+    own_ref = pltpu.make_async_copy(ref_ref.at[x], rbuf.at[bo, x], r_recv.at[bo, x])
     own_gen.start()
     own_ref.start()
 
-    for i in range(inner):
+    for step in range(inner):
+        i = lax.rem(bi + step, inner)
         for h in range(halves):
             pltpu.make_async_copy(gen_ref.at[0], gbuf.at[i, h], g_recv.at[i, h]).wait()
-    for i in range(inner):
         points = jnp.concatenate([gbuf[i, h] for h in range(halves)], axis=1)
         norm = jnp.sum(points * points, axis=0, keepdims=True)
-        rows[pl.ds(i * n, n), :] = gen_rows(points, norm)
+        rows[pl.ds(pl.multiple_of(i * n, n), n), :] = gen_rows(points, norm)
         if vec:
             for c, wide in enumerate(spread_gen(points[:, n - vec :], norm[:, n - vec :])):
                 wide_gen[i, c] = wide
@@ -153,7 +158,7 @@
     def some_refs(step, carry):
         o = lax.rem(bo + step, outer)
         for h in range(halves):
-            pltpu.make_async_copy(ref_ref.at[pl.ds(0, chunk)], rbuf.at[o, h], r_recv.at[o, h]).wait()
+            pltpu.make_async_copy(ref_ref.at[0], rbuf.at[o, h], r_recv.at[o, h]).wait()
 
         def one_ref(c, carry):
             points = jnp.concatenate([rbuf[o, h, c] for h in range(halves)], axis=1)
@@ -219,6 +224,8 @@
         in_specs=[pl.BlockSpec(memory_space=pltpu.VMEM)] * 2,
         out_specs=pl.BlockSpec(memory_space=pltpu.VMEM),
         scratch_shapes=[
+            pltpu.VMEM((1, 3, share), jnp.float32),
+            pltpu.VMEM((halves, chunk, 3, share), jnp.float32),
             pltpu.VMEM((inner, halves, 3, share), jnp.float32),
             pltpu.VMEM((outer, halves, chunk, 3, share), jnp.float32),
             pltpu.VMEM((inner * n, 128), jnp.bfloat16),
@@ -235,7 +242,7 @@
         ],
         compiler_params=pltpu.CompilerParams(collective_id=0, has_side_effects=True),
         name="chamfer",
-    )(gen_points, ref_points)
+    )(jnp.transpose(gen_points, (1, 0, 2)), jnp.transpose(ref_points, (1, 0, 2)))
 
 
 def solution(mesh):

time: 58.2 us -> 55.5 us (0.954)
  local copies, waits for them, and re-layouts: 3.86 us -> 1.19 us
    unnamed x3 -> x1, local copies, waits for them, and re-layouts: 3.86 us -> 1.19 us
where the time goes in v2:
time: 55.5 us; the launch traced here: 55.4 us
  Pallas kernels  54.2 us (98%)
  local copies, waits for them, and re-layouts  1.19 us (2%)
    pallas_call x1, Pallas kernels, shards(): pl.pallas_call(functools.partial(kernel, sizes), out_shape=jax.ShapeDtype...  54.2 us
    unnamed x1, local copies, waits for them, and re-layouts  1.19 us

profile of v2, /device:TPU:0, one launch (start us, length us, event | category | flops | bytes accessed | tf_op | source)
XLA Modules:
  0.0 55.4 jit_solution(13990678722341226367)
XLA Ops:
  0.0 54.2 %chamfer.1 = f32[1,128]{1,0:T(1,128)} custom-call(f32[3,1,512]{2,1,0:T(1,128)} %bitcast.3, f32[3,8,512]{2,1,0:T(8,128)} %bitcast.2), custom_call_target="tpu_custom_call" | custom-call | tf_op jit(solution)/shard_map/chamfer/pallas_call | solution.py:221
  54.2 1.2 %copy.4 = f32[1,128]{1,0:T(1,128)} copy(f32[1,128]{1,0:T(1,128)} %chamfer.1) | data formatting | bytes 1024
